TPU v7x, 128 devices: a whole 4x4x4 slice. The times are simulated.
128 devices in a mesh: brick: 8 (over y, core), grp: 16 (over x, z).
Axes of the slice: x: 4, y: 4, z: 4, core: 2. Of those that a mesh axis runs over, the one named last changes fastest.
Arguments:
- source: float32 [16, 8, 2, 32, 1024], P('grp', 'brick'), may hold values from -21 to 21
- uptake: float32 [16, 8, 2, 32, 1024], P('grp', 'brick'), may hold values from 0.00015 to 0.006
- conductance: float32 [16, 8, 6, 2, 32, 1024], P('grp', 'brick'), may hold values from 0 to 3, as said below
- occupancy: int32 [16, 2, 8], replicated, may hold values from 0 to 1, as said below
- assignment: int32 [8], replicated, may hold values from 0 to 7, as said below
Outputs:
- solution_field: float32 [16, 8, 2, 32, 1024], P('grp', 'brick')
- residual: float32 [16, 8, 2, 32, 1024], P('grp', 'brick')
Inputs may be any that keep to these rules, and one draw needn't show every extreme that they name: `occupancy`: 1 marks an occupied brick; in every draw one patch of some slab has all its bricks occupied. `assignment`: each patch is held by exactly one index of brick. `conductance`: equal at both ends of a bond: the value toward +x at a cell is the value toward -x at its +x neighbour, likewise for y and z, the lattice being read cyclically; values toward +z and -z are 0.3 or more.
All inputs are finite; a program needn't handle non-finite values.
Results may differ from a plain program's by a relative error of at most 0.0003.
Values sent between devices are 32-bit elements; how exact they have to be, the bound alone decides.
A program may use at most 128 MiB of HBM per device.

v0:
```python
import jax
import jax.numpy as jnp
from jax import lax
from jax.sharding import PartitionSpec as P

BS = 32
PATCH_X = 1
PATCH_Y = 2
ITERS = 3
OMEGA = 0.6


def extended_2(block, sides, width):
    for axis, dim in sides:
        count = lax.axis_size(axis)
        forward = [(i, i + 1) for i in range(count - 1)]
        backward = [(target, source) for source, target in forward]
        low = lax.ppermute(
            lax.slice_in_dim(block, block.shape[dim] - width, None, axis=dim), axis, forward
        )
        high = lax.ppermute(lax.slice_in_dim(block, 0, width, axis=dim), axis, backward)
        block = jnp.concatenate([low, block, high], axis=dim)
    return block


def assemble(coarse_diag, couplings, strides):
    extent = coarse_diag.shape[0]
    matrix = jnp.diag(coarse_diag)
    for coupling, stride in zip(couplings, strides):
        banded = coupling[: extent - stride]
        matrix = matrix - jnp.diag(banded, stride) - jnp.diag(banded, -stride)
    return matrix


def pad_rows(block, capacity):
    return jnp.pad(block, ((0, capacity - block.shape[0]), (0, 0)))


def on_device(source, uptake, conductance, occupancy, assignment):
    face_size = BS * BS
    capacity = max(PATCH_X, PATCH_Y)
    slot_count = PATCH_X * PATCH_Y
    slab_index = lax.axis_index("grp")
    brick_index = lax.axis_index("brick")
    brick_count = lax.axis_size("brick")
    across = brick_count // 2
    peer_ids = jnp.arange(brick_count, dtype=jnp.int32)
    patch_index = assignment[brick_index]
    patch_row = patch_index // across
    patch_column = patch_index % across

    def owner_of(row_shift, column_shift):
        row_target = patch_row + row_shift
        column_target = patch_column + column_shift
        inside = (
            (row_target >= 0) & (row_target < 2) & (column_target >= 0) & (column_target < across)
        )
        holder = jnp.sum(jnp.where(assignment == row_target * across + column_target, peer_ids, 0))
        return jnp.where(inside, holder, -1)

    wanted = jnp.stack([owner_of(1, 0), owner_of(-1, 0), owner_of(0, 1), owner_of(0, -1)])
    padded = jnp.pad(occupancy, 1)
    window = lax.dynamic_slice(
        padded,
        (slab_index, patch_row * PATCH_X, patch_column * PATCH_Y),
        (3, PATCH_X + 2, PATCH_Y + 2),
    ).astype(jnp.float32)
    centre = window[1, 1:-1, 1:-1].reshape(slot_count)
    toward = [
        window[1, 2:, 1:-1],
        window[1, :-2, 1:-1],
        window[1, 1:-1, 2:],
        window[1, 1:-1, :-2],
        window[2, 1:-1, 1:-1],
        window[0, 1:-1, 1:-1],
    ]
    first_axis = lax.broadcasted_iota(jnp.int32, (1, BS, face_size), 1)
    flat_axis = lax.broadcasted_iota(jnp.int32, (1, BS, face_size), 2)
    second_axis = flat_axis // BS
    third_axis = flat_axis % BS
    cube_third = lax.broadcasted_iota(jnp.int32, (1, BS, BS, BS), 3)
    borders = [
        first_axis == BS - 1,
        first_axis == 0,
        second_axis == BS - 1,
        second_axis == 0,
        third_axis == BS - 1,
        third_axis == 0,
    ]
    bonds = conductance[0, 0]
    live_here = centre[:, None, None]
    effective = []
    for direction in range(6):
        neighbour_live = toward[direction].reshape(slot_count)[:, None, None]
        active = jnp.where(borders[direction], live_here * neighbour_live, live_here)
        effective.append(bonds[direction] * active)
    absorb = uptake[0, 0]
    diagonal = absorb
    for direction in range(6):
        diagonal = diagonal + effective[direction]

    def apply_operator(field):
        lower_x = field[:, 0, :]
        upper_x = field[:, BS - 1, :]
        lower_y = field[:, :, :BS].reshape(slot_count, face_size)
        upper_y = field[:, :, face_size - BS :].reshape(slot_count, face_size)
        cube = field.reshape(slot_count, BS, BS, BS)
        lower_z = cube[:, :, :, 0].reshape(slot_count, face_size)
        upper_z = cube[:, :, :, BS - 1].reshape(slot_count, face_size)
        grid_lower_x = lower_x.reshape(PATCH_X, PATCH_Y, face_size)
        grid_upper_x = upper_x.reshape(PATCH_X, PATCH_Y, face_size)
        grid_lower_y = lower_y.reshape(PATCH_X, PATCH_Y, face_size)
        grid_upper_y = upper_y.reshape(PATCH_X, PATCH_Y, face_size)
        outgoing_sides = jnp.stack(
            [
                pad_rows(grid_lower_x[0], capacity),
                pad_rows(grid_upper_x[PATCH_X - 1], capacity),
                pad_rows(grid_lower_y[:, 0], capacity),
                pad_rows(grid_upper_y[:, PATCH_Y - 1], capacity),
            ]
        )
        portion = lax.all_gather(outgoing_sides[None], "brick", axis=0, tiled=True)
        sources = jnp.arange(portion.shape[0], dtype=jnp.int32)
        matches = sources[:, None] == wanted[None, :]
        remote = jnp.zeros((4, capacity, face_size), jnp.float32) + jnp.sum(
            jnp.where(matches[:, :, None, None], portion, 0.0), axis=0
        )
        stacked = jnp.stack([lower_z, upper_z])
        extended = extended_2(stacked, (("grp", 0),), 1)
        from_below = extended[0].reshape(slot_count, BS, BS, 1)
        from_above = extended[3].reshape(slot_count, BS, BS, 1)
        beyond_xplus = jnp.concatenate(
            [grid_lower_x[1:], remote[0, :PATCH_Y][None]], axis=0
        ).reshape(slot_count, face_size)
        beyond_xminus = jnp.concatenate(
            [remote[1, :PATCH_Y][None], grid_upper_x[:-1]], axis=0
        ).reshape(slot_count, face_size)
        beyond_yplus = jnp.concatenate(
            [grid_lower_y[:, 1:], remote[2, :PATCH_X][:, None]], axis=1
        ).reshape(slot_count, BS, BS)
        beyond_yminus = jnp.concatenate(
            [remote[3, :PATCH_X][:, None], grid_upper_y[:, :-1]], axis=1
        ).reshape(slot_count, BS, BS)
        upper_neighbour = jnp.where(
            cube_third == BS - 1, from_above, jnp.roll(cube, -1, axis=3)
        ).reshape(slot_count, BS, face_size)
        lower_neighbour = jnp.where(cube_third == 0, from_below, jnp.roll(cube, 1, axis=3)).reshape(
            slot_count, BS, face_size
        )
        total = diagonal * field
        total = total - effective[0] * jnp.concatenate(
            [field[:, 1:, :], beyond_xplus[:, None, :]], axis=1
        )
        total = total - effective[1] * jnp.concatenate(
            [beyond_xminus[:, None, :], field[:, :-1, :]], axis=1
        )
        total = total - effective[2] * jnp.concatenate([field[:, :, BS:], beyond_yplus], axis=2)
        total = total - effective[3] * jnp.concatenate(
            [beyond_yminus, field[:, :, : face_size - BS]], axis=2
        )
        total = total - effective[4] * upper_neighbour
        total = total - effective[5] * lower_neighbour
        return total

    slot_ids = jnp.arange(slot_count)
    brick_first = slot_ids // PATCH_Y
    brick_second = slot_ids % PATCH_Y
    inside = [
        (brick_first < PATCH_X - 1).astype(jnp.float32),
        (brick_first > 0).astype(jnp.float32),
        (brick_second < PATCH_Y - 1).astype(jnp.float32),
        (brick_second > 0).astype(jnp.float32),
    ]
    face_sums = [
        jnp.sum(effective[0][:, BS - 1, :], axis=1),
        jnp.sum(effective[1][:, 0, :], axis=1),
        jnp.sum(effective[2][:, :, face_size - BS :], axis=(1, 2)),
        jnp.sum(effective[3][:, :, :BS], axis=(1, 2)),
        jnp.sum(effective[4].reshape(slot_count, BS, BS, BS)[:, :, :, BS - 1], axis=(1, 2)),
        jnp.sum(effective[5].reshape(slot_count, BS, BS, BS)[:, :, :, 0], axis=(1, 2)),
    ]
    coarse_diag = jnp.sum(absorb, axis=(1, 2))
    for direction in range(4):
        coarse_diag = coarse_diag + face_sums[direction] * inside[direction]
    coarse_diag = coarse_diag + face_sums[4] + face_sums[5]
    grp_count = lax.axis_size("grp")
    grp_ids = jnp.arange(grp_count, dtype=jnp.int32)

    def butterfly(values, axes):
        for axis in axes:
            count = lax.axis_size(axis)
            if count & count - 1:
                values = lax.psum(values, axis)
                continue
            stride = 1
            while stride < count:
                pairs = [(i, i ^ stride) for i in range(count)]
                values = values + lax.ppermute(values, axis, pairs)
                stride *= 2
        return values

    def slab_slot(values):
        here = (grp_ids == slab_index).astype(jnp.float32)
        return here[:, None, None] * values[None]

    forcing = source[0, 0] * live_here
    record = jnp.stack(
        [
            coarse_diag,
            face_sums[0] * inside[0],
            face_sums[2] * inside[2],
            face_sums[4],
            jnp.sum(forcing, axis=(1, 2)),
        ]
    )
    gathered = butterfly(slab_slot(record), ("grp",))
    columns = jnp.transpose(gathered, (1, 0, 2)).reshape(5, -1)
    matrix = assemble(columns[0], (columns[1], columns[2], columns[3]), (PATCH_Y, 1, slot_count))
    factor = jnp.linalg.cholesky(matrix)

    def coarse_solve(terms):
        middle = lax.linalg.triangular_solve(factor, terms[:, None], left_side=True, lower=True)
        result = lax.linalg.triangular_solve(
            factor, middle, left_side=True, lower=True, transpose_a=True
        )
        return lax.dynamic_slice_in_dim(result[:, 0], slab_index * slot_count, slot_count)

    def precondition(residual_field, terms):
        smoothed = OMEGA * residual_field / diagonal
        smoothed = smoothed + OMEGA * (residual_field - apply_operator(smoothed)) / diagonal
        return smoothed + coarse_solve(terms)[:, None, None]

    brick_here = (peer_ids == brick_index).astype(jnp.float32)

    def dot_and_sums(product, field):
        sums = slab_slot(jnp.sum(field, axis=(1, 2))[None])[:, 0]
        spread = brick_here[:, None, None] * sums[None]
        packed = jnp.concatenate([jnp.sum(product)[None], spread.reshape(-1)])
        total = butterfly(packed, ("brick", "grp"))
        mine = lax.dynamic_index_in_dim(
            total[1:].reshape(brick_count, -1), brick_index, keepdims=False
        )
        return (total[0], mine)

    def global_sum(values):
        return butterfly(jnp.sum(values)[None], ("brick", "grp"))[0]

    terms = columns[4]
    solution_field = jnp.zeros_like(forcing)
    residual = forcing
    search = precondition(residual, terms)
    energy = global_sum(residual * search)
    for iteration in range(ITERS):
        mapped = apply_operator(search)
        curvature, mapped_terms = dot_and_sums(search * mapped, mapped)
        step_size = energy / curvature
        solution_field = solution_field + step_size * search
        residual = residual - step_size * mapped
        if iteration + 1 < ITERS:
            terms = terms - step_size * mapped_terms
            smoothed = precondition(residual, terms)
            renewed = global_sum(residual * smoothed)
            search = smoothed + renewed / energy * search
            energy = renewed
    return (solution_field[None, None], residual[None, None])


def solution(mesh):
    return jax.shard_map(
        on_device,
        mesh=mesh,
        in_specs=(
            P("grp", "brick", None, None, None),
            P("grp", "brick", None, None, None),
            P("grp", "brick", None, None, None, None),
            P(),
            P(),
        ),
        out_specs=(P("grp", "brick", None, None, None), P("grp", "brick", None, None, None)),
        check_vma=False,
    )
```

profile of v0, /device:TPU:0, one launch (start us, length us, event | category | flops | bytes accessed | tf_op | source)
XLA Modules:
  0.0 795.7 jit_solution(16637626487733563843)
XLA Ops:
  31.3 5.5 multiply_divide_fusion.2
  62.5 13.4 %all-gather = f32[32,2,1024]{2,1,0:T(2,128)S(1)} all-gather(f32[4,2,1024]{2,1,0:T(2,128)S(1)} %copy.421), channel_id=2, replica_groups=mesh['brick'=8,'grp'=16] {'brick'}, dimensions={0}, use_global_device_ids=true | all-gather | bytes 294912 | tf_op jit(solution)/shard_map/all_gather | solution.py:122
  84.2 5.6 collective-permute-start.3
  121.3 8.5 %fusion.46 = (f32[2,32,32,32]{3,2,1,0:T(8,128)S(1)}, f32[2,32,32,32]{3,2,1,0:T(8,128)}, f32[2,32,32,32]{3,2,1,0:T(8,128)}) fusion(f32[2,32,32,32]{3,2,1,0:T(8,128)} %get-tuple-element.73, f32[2,32,32,32]{3,2,1,0:T(8,128)} %copy-done.15, f32[2,32,32,32]{3,2,1,0:T(8,128)} %copy-done.14, f32[2,32,32,32]{3,2,1,0:T(8,128)} %concatenate.668, ...), kind=kLoop, calls=%fused_computation.88 | loop fusion | flops 2293760 | bytes 4538480 | tf_op jit(solution)/shard_map/add | solution.py:231
  152.9 12.8 %all-gather.1 = f32[32,2,1024]{2,1,0:T(2,128)S(1)} all-gather(f32[4,2,1024]{2,1,0:T(2,128)S(1)} %copy.424), channel_id=3, replica_groups=mesh['brick'=8,'grp'=16] {'brick'}, dimensions={0}, use_global_device_ids=true | all-gather | bytes 294912 | tf_op jit(solution)/shard_map/all_gather | solution.py:122
  206.9 3.8 multiply_reduce_fusion.4
  235.4 4.4 collective-permute-start.20
  270.3 3.7 collective-permute-done.10
  278.8 3.7 collective-permute-start.12
  296.8 13.2 %all-gather.2 = f32[32,2,1024]{2,1,0:T(2,128)S(1)} all-gather(f32[4,2,1024]{2,1,0:T(2,128)S(1)} %copy.430), channel_id=4, replica_groups=mesh['brick'=8,'grp'=16] {'brick'}, dimensions={0}, use_global_device_ids=true | all-gather | bytes 294912 | tf_op jit(solution)/shard_map/all_gather | solution.py:122
  315.7 6.9 multiply_divide_fusion.1
  372.2 3.8 multiply_reduce_fusion.3
  391.8 4.0 collective-permute-start.27
  396.5 3.8 collective-permute-start.28
  402.3 5.7 collective-permute-start.29
  408.8 4.9 collective-permute-start.30
  417.2 13.0 %all-gather.3 = f32[32,2,1024]{2,1,0:T(2,128)S(1)} all-gather(f32[4,2,1024]{2,1,0:T(2,128)S(1)} %copy.435), channel_id=5, replica_groups=mesh['brick'=8,'grp'=16] {'brick'}, dimensions={0}, use_global_device_ids=true | all-gather | bytes 294912 | tf_op jit(solution)/shard_map/all_gather | solution.py:122
  434.1 6.3 multiply_add_fusion.1
  486.5 4.1 collective-permute-start.37
  492.2 5.5 collective-permute-start.38
  499.9 3.6 collective-permute-start.39
  517.4 13.1 %all-gather.4 = f32[32,2,1024]{2,1,0:T(2,128)S(1)} all-gather(f32[4,2,1024]{2,1,0:T(2,128)S(1)} %copy.440), channel_id=6, replica_groups=mesh['brick'=8,'grp'=16] {'brick'}, dimensions={0}, use_global_device_ids=true | all-gather | bytes 294912 | tf_op jit(solution)/shard_map/all_gather | solution.py:122
  535.4 6.6 multiply_divide_fusion
  589.0 3.9 multiply_reduce_fusion.1
  608.9 4.0 collective-permute-start.45
  619.7 4.9 collective-permute-start.47
  625.6 4.0 collective-permute-start.48
  641.0 13.2 %all-gather.5 = f32[32,2,1024]{2,1,0:T(2,128)S(1)} all-gather(f32[4,2,1024]{2,1,0:T(2,128)S(1)} %copy.445), channel_id=7, replica_groups=mesh['brick'=8,'grp'=16] {'brick'}, dimensions={0}, use_global_device_ids=true | all-gather | bytes 294912 | tf_op jit(solution)/shard_map/all_gather | solution.py:122
  659.3 9.3 %multiply_add_fusion = f32[2,32,32,32]{3,2,1,0:T(8,128)S(1)} fusion(f32[2,32,32,32]{3,2,1,0:T(8,128)} %copy-done.16, f32[2,32,32,32]{3,2,1,0:T(8,128)} %get-tuple-element.73, f32[2,32,32,32]{3,2,1,0:T(8,128)} %copy-done.15, f32[2,32,32,32]{3,2,1,0:T(8,128)} %copy-done.14, f32[2,32,32,32]{3,2,1,0:T(8,128)} %concatenate.784, ...), kind=kLoop, calls=%fused_computation.76 | loop fusion | flops 3735552 | bytes 5865592 | tf_op jit(solution)/shard_map/add | solution.py:263
  713.5 3.8 collective-permute-start.55
  740.0 3.9 fusion.96
  788.8 5.9 fusion.148
  (970 shorter events, 561.3 us)
Async XLA Ops:
  40.5 42.8 %collective-permute-start.2 = (f32[16,5,2]{2,0,1:T(8,128)}, f32[16,5,2]{2,0,1:T(8,128)}, u32[]{:S(2)}, u32[]{:S(2)}) collective-permute-start(f32[16,5,2]{2,0,1:T(8,128)} %broadcast_multiply_fusion.3), channel_id=1, source_target_pairs={{0,1},{1,0},{2,3},{3,2},{4,5},{5,4},{6,7},{7,6},{8,9},{9,8},{10,11... | collective-permute-start | bytes 1928 | tf_op jit(solution)/shard_map/ppermute | solution.py:198
  46.3 74.2 %collective-permute-start.1 = (f32[1,2,1024]{2,1,0:T(2,128)}, f32[1,2,1024]{2,1,0:T(2,128)}, u32[]{:S(2)}, u32[]{:S(2)}) collective-permute-start(f32[1,2,1024]{2,1,0:T(2,128)} %stack_reshape_squeeze.37), channel_id=1, source_target_pairs={{0,1},{1,2},{2,3},{3,4},{4,5},{5,6},{6,7},{7,8},{8,9},{9,10},{10,1... | collective-permute-start | bytes 24584 | tf_op jit(solution)/shard_map/ppermute | solution.py:18
  50.3 69.5 %collective-permute-start = (f32[1,2,1024]{2,1,0:T(2,128)}, f32[1,2,1024]{2,1,0:T(2,128)}, u32[]{:S(2)}, u32[]{:S(2)}) collective-permute-start(f32[1,2,1024]{2,1,0:T(2,128)} %stack_reshape_squeeze.36), channel_id=1, source_target_pairs={{1,0},{2,1},{3,2},{4,3},{5,4},{6,5},{7,6},{8,7},{9,8},{10,9},{11,1... | collective-permute-start | bytes 24584 | tf_op jit(solution)/shard_map/ppermute | solution.py:21
  84.2 7.6 collective-permute-start.3
  92.7 9.4 %collective-permute-start.4 = (f32[16,5,2]{2,0,1:T(8,128)S(1)}, f32[16,5,2]{2,0,1:T(8,128)S(1)}, u32[]{:S(2)}, u32[]{:S(2)}) collective-permute-start(f32[16,5,2]{2,0,1:T(8,128)S(1)} %fusion.258), channel_id=1, source_target_pairs={{0,4},{1,5},{2,6},{3,7},{4,0},{5,1},{6,2},{7,3},{8,12},{9,13},{10,... | collective-permute-start | bytes 1928 | tf_op jit(solution)/shard_map/ppermute | solution.py:198
  102.1 9.6 %collective-permute-start.5 = (f32[16,5,2]{2,0,1:T(8,128)S(1)}, f32[16,5,2]{2,0,1:T(8,128)S(1)}, u32[]{:S(2)}, u32[]{:S(2)}) collective-permute-start(f32[16,5,2]{2,0,1:T(8,128)S(1)} %add.671), channel_id=1, source_target_pairs={{0,8},{1,9},{2,10},{3,11},{4,12},{5,13},{6,14},{7,15},{8,0},{9,1},... | collective-permute-start | bytes 1928 | tf_op jit(solution)/shard_map/ppermute | solution.py:198
  176.7 18.5 %collective-permute-start.14 = (f32[1,2,1024]{2,1,0:T(2,128)}, f32[1,2,1024]{2,1,0:T(2,128)}, u32[]{:S(2)}, u32[]{:S(2)}) collective-permute-start(f32[1,2,1024]{2,1,0:T(2,128)} %stack_reshape_squeeze.39), channel_id=1, source_target_pairs={{0,1},{1,2},{2,3},{3,4},{4,5},{5,6},{6,7},{7,8},{8,9},{9,10},{10,1... | collective-permute-start | bytes 24584 | tf_op jit(solution)/shard_map/ppermute | solution.py:18
  178.6 22.5 %collective-permute-start.13 = (f32[1,2,1024]{2,1,0:T(2,128)}, f32[1,2,1024]{2,1,0:T(2,128)}, u32[]{:S(2)}, u32[]{:S(2)}) collective-permute-start(f32[1,2,1024]{2,1,0:T(2,128)} %stack_reshape_squeeze.38), channel_id=1, source_target_pairs={{1,0},{2,1},{3,2},{4,3},{5,4},{6,5},{7,6},{8,7},{9,8},{10,9},{11,1... | collective-permute-start | bytes 24584 | tf_op jit(solution)/shard_map/ppermute | solution.py:21
  235.4 16.3 %collective-permute-start.20 = (f32[257]{0:T(512)}, f32[257]{0:T(512)}, u32[]{:S(2)}, u32[]{:S(2)}) collective-permute-start(f32[257]{0:T(512)} %add.700), channel_id=1, source_target_pairs={{0,4},{1,5},{2,6},{3,7},{4,0},{5,1},{6,2},{7,3},{8,12},{9,13},{10,... | collective-permute-start | bytes 3092 | tf_op jit(solution)/shard_map/ppermute | solution.py:198
  247.0 6.6 collective-permute-start.6
  252.4 32.1 %collective-permute-start.21 = (f32[257]{0:T(512)S(1)}, f32[257]{0:T(512)S(1)}, u32[]{:S(2)}, u32[]{:S(2)}) collective-permute-start(f32[257]{0:T(512)S(1)} %add.701), channel_id=1, source_target_pairs={{0,8},{1,9},{2,10},{3,11},{4,12},{5,13},{6,14},{7,15},{8,0},{9,1},... | collective-permute-start | bytes 3092 | tf_op jit(solution)/shard_map/ppermute | solution.py:198
  332.4 28.0 %collective-permute-start.23 = (f32[1,2,1024]{2,1,0:T(2,128)}, f32[1,2,1024]{2,1,0:T(2,128)}, u32[]{:S(2)}, u32[]{:S(2)}) collective-permute-start(f32[1,2,1024]{2,1,0:T(2,128)} %stack_reshape_squeeze.41), channel_id=1, source_target_pairs={{0,1},{1,2},{2,3},{3,4},{4,5},{5,6},{6,7},{7,8},{8,9},{9,10},{10,1... | collective-permute-start | bytes 24584 | tf_op jit(solution)/shard_map/ppermute | solution.py:18
  334.9 31.4 %collective-permute-start.22 = (f32[1,2,1024]{2,1,0:T(2,128)}, f32[1,2,1024]{2,1,0:T(2,128)}, u32[]{:S(2)}, u32[]{:S(2)}) collective-permute-start(f32[1,2,1024]{2,1,0:T(2,128)} %stack_reshape_squeeze.40), channel_id=1, source_target_pairs={{1,0},{2,1},{3,2},{4,3},{5,4},{6,5},{7,6},{8,7},{9,8},{10,9},{11,1... | collective-permute-start | bytes 24584 | tf_op jit(solution)/shard_map/ppermute | solution.py:21
  402.3 5.9 collective-permute-start.29
  408.8 5.1 collective-permute-start.30
  444.3 13.6 %collective-permute-start.32 = (f32[1,2,1024]{2,1,0:T(2,128)S(1)}, f32[1,2,1024]{2,1,0:T(2,128)S(1)}, u32[]{:S(2)}, u32[]{:S(2)}) collective-permute-start(f32[1,2,1024]{2,1,0:T(2,128)S(1)} %stack_reshape_squeeze.43), channel_id=1, source_target_pairs={{0,1},{1,2},{2,3},{3,4},{4,5},{5,6},{6,7},{7,8},{8,9},{9,10},{10,1... | collective-permute-start | bytes 24584 | tf_op jit(solution)/shard_map/ppermute | solution.py:18
  446.3 16.3 %collective-permute-start.31 = (f32[1,2,1024]{2,1,0:T(2,128)}, f32[1,2,1024]{2,1,0:T(2,128)}, u32[]{:S(2)}, u32[]{:S(2)}) collective-permute-start(f32[1,2,1024]{2,1,0:T(2,128)} %stack_reshape_squeeze.42), channel_id=1, source_target_pairs={{1,0},{2,1},{3,2},{4,3},{5,4},{6,5},{7,6},{8,7},{9,8},{10,9},{11,1... | collective-permute-start | bytes 24584 | tf_op jit(solution)/shard_map/ppermute | solution.py:21
  486.5 5.7 collective-permute-start.37
  492.2 7.1 collective-permute-start.38
  499.9 12.6 %collective-permute-start.39 = (f32[257]{0:T(512)}, f32[257]{0:T(512)}, u32[]{:S(2)}, u32[]{:S(2)}) collective-permute-start(f32[257]{0:T(512)} %add.733), channel_id=1, source_target_pairs={{0,8},{1,9},{2,10},{3,11},{4,12},{5,13},{6,14},{7,15},{8,0},{9,1},... | collective-permute-start | bytes 3092 | tf_op jit(solution)/shard_map/ppermute | solution.py:198
  551.6 25.7 %collective-permute-start.41 = (f32[1,2,1024]{2,1,0:T(2,128)}, f32[1,2,1024]{2,1,0:T(2,128)}, u32[]{:S(2)}, u32[]{:S(2)}) collective-permute-start(f32[1,2,1024]{2,1,0:T(2,128)} %stack_reshape_squeeze.45), channel_id=1, source_target_pairs={{0,1},{1,2},{2,3},{3,4},{4,5},{5,6},{6,7},{7,8},{8,9},{9,10},{10,1... | collective-permute-start | bytes 24584 | tf_op jit(solution)/shard_map/ppermute | solution.py:18
  554.1 29.1 %collective-permute-start.40 = (f32[1,2,1024]{2,1,0:T(2,128)}, f32[1,2,1024]{2,1,0:T(2,128)}, u32[]{:S(2)}, u32[]{:S(2)}) collective-permute-start(f32[1,2,1024]{2,1,0:T(2,128)} %stack_reshape_squeeze.44), channel_id=1, source_target_pairs={{1,0},{2,1},{3,2},{4,3},{5,4},{6,5},{7,6},{8,7},{9,8},{10,9},{11,1... | collective-permute-start | bytes 24584 | tf_op jit(solution)/shard_map/ppermute | solution.py:21
  603.1 5.2 collective-permute-start.44
  613.9 5.2 collective-permute-start.46
  619.7 5.3 collective-permute-start.47
  625.6 5.2 collective-permute-start.48
  672.8 12.3 %collective-permute-start.50 = (f32[1,2,1024]{2,1,0:T(2,128)S(1)}, f32[1,2,1024]{2,1,0:T(2,128)S(1)}, u32[]{:S(2)}, u32[]{:S(2)}) collective-permute-start(f32[1,2,1024]{2,1,0:T(2,128)S(1)} %stack_reshape_squeeze.47), channel_id=1, source_target_pairs={{0,1},{1,2},{2,3},{3,4},{4,5},{5,6},{6,7},{7,8},{8,9},{9,10},{10,1... | collective-permute-start | bytes 24584 | tf_op jit(solution)/shard_map/ppermute | solution.py:18
  675.2 14.0 %collective-permute-start.49 = (f32[1,2,1024]{2,1,0:T(2,128)}, f32[1,2,1024]{2,1,0:T(2,128)}, u32[]{:S(2)}, u32[]{:S(2)}) collective-permute-start(f32[1,2,1024]{2,1,0:T(2,128)} %stack_reshape_squeeze.46), channel_id=1, source_target_pairs={{1,0},{2,1},{3,2},{4,3},{5,4},{6,5},{7,6},{8,7},{9,8},{10,9},{11,1... | collective-permute-start | bytes 24584 | tf_op jit(solution)/shard_map/ppermute | solution.py:21
  704.2 5.1 collective-permute-start.53
  713.5 23.9 %collective-permute-start.55 = (f32[257]{0:T(512)S(1)}, f32[257]{0:T(512)S(1)}, u32[]{:S(2)}, u32[]{:S(2)}) collective-permute-start(f32[257]{0:T(512)S(1)} %add.759), channel_id=1, source_target_pairs={{0,2},{1,3},{2,0},{3,1},{4,6},{5,7},{6,4},{7,5},{8,10},{9,11},{10,... | collective-permute-start | bytes 3092 | tf_op jit(solution)/shard_map/ppermute | solution.py:198
  738.0 12.3 %collective-permute-start.56 = (f32[257]{0:T(512)}, f32[257]{0:T(512)}, u32[]{:S(2)}, u32[]{:S(2)}) collective-permute-start(f32[257]{0:T(512)} %add.760), channel_id=1, source_target_pairs={{0,4},{1,5},{2,6},{3,7},{4,0},{5,1},{6,2},{7,3},{8,12},{9,13},{10,... | collective-permute-start | bytes 3092 | tf_op jit(solution)/shard_map/ppermute | solution.py:198
  751.7 35.1 %collective-permute-start.57 = (f32[257]{0:T(512)}, f32[257]{0:T(512)}, u32[]{:S(2)}, u32[]{:S(2)}) collective-permute-start(f32[257]{0:T(512)} %add.761), channel_id=1, source_target_pairs={{0,8},{1,9},{2,10},{3,11},{4,12},{5,13},{6,14},{7,15},{8,0},{9,1},... | collective-permute-start | bytes 3092 | tf_op jit(solution)/shard_map/ppermute | solution.py:198
  (253 other events, 2053.4 us)
where the time goes:
time: 810 us; the launch traced here: 796 us
  local copies, waits for them, and re-layouts  344 us (42%)
  other arithmetic  145 us (18%)
  starting transfers between devices  145 us (18%)
  blocking collectives  78.8 us (10%)
  waiting for transfers between devices  54 us (7%)
  between operations  25.7 us (3%)
    ppermute x46, starting transfers between devices, butterfly(): values = values + lax.ppermute(values, axis, pairs)  124 us
    all_gather x6, blocking collectives, apply_operator(): portion = lax.all_gather(outgoing_sides[None], 'brick', axis=0, tiled=True)  78.8 us
    ppermute x46, waiting for transfers between devices, butterfly(): values = values + lax.ppermute(values, axis, pairs)  54 us
    broadcast_in_dim x26, local copies, waits for them, and re-layouts, apply_operator(): jnp.where(cube_third == BS - 1, from_above, jnp.roll(cube, -1, axis=3))  46.7 us
    broadcast_in_dim x26, local copies, waits for them, and re-layouts, apply_operator(): jnp.where(cube_third == 0, from_below, jnp.roll(cube, 1, axis=3))  42.9 us
    concatenate x12, local copies, waits for them, and re-layouts, apply_operator(): jnp.roll(cube, 1, axis=3)  25.5 us
    concatenate x12, local copies, waits for them, and re-layouts, apply_operator(): jnp.roll(cube, -1, axis=3)  23 us
    concatenate x15, local copies, waits for them, and re-layouts, apply_operator(): jnp.concatenate([field[:, :, BS:], beyond_yplus], axis=2)  21.9 us
  transfers between devices with their start and end apart: 58, of which 34 were waited for; matrix products, arithmetic and copies ran while one was open for 30% of the time, Pallas kernels for 0%

commit v1 on v0

--- a/solution.py
+++ b/solution.py
@@ -119,7 +119,12 @@
                 pad_rows(grid_upper_y[:, PATCH_Y - 1], capacity),
             ]
         )
-        portion = lax.all_gather(outgoing_sides[None], "brick", axis=0, tiled=True)
+        portion = jnp.concatenate(
+            lax.all_to_all(
+                jnp.stack([outgoing_sides[None]] * lax.axis_size("brick")), "brick", 0, 0
+            ),
+            axis=0,
+        )
         sources = jnp.arange(portion.shape[0], dtype=jnp.int32)
         matches = sources[:, None] == wanted[None, :]
         remote = jnp.zeros((4, capacity, face_size), jnp.float32) + jnp.sum(

time: 810 us -> 758 us (0.936)
  blocking collectives: 78.8 us -> 0 us
  starting transfers between devices: 145 us -> 188 us
  local copies, waits for them, and re-layouts: 344 us -> 329 us
  waiting for transfers between devices: 54 us -> 42.6 us
  other arithmetic: 145 us -> 154 us
    all_gather x6 -> x0, blocking collectives: 78.8 us -> none  [apply_operator(): portion = lax.all_gather(outgoing_sides[None], 'brick', axis=0, tiled=True)]
    all_to_all x0 -> x6, starting transfers between devices: none -> 28.6 us  [apply_operator(): lax.all_to_all(jnp.stack([outgoing_sides[None]] * lax.axis_size('brick'))...]
    ppermute x46, starting transfers between devices: 124 us -> 139 us  [butterfly(): values = values + lax.ppermute(values, axis, pairs)]
    ppermute x46, waiting for transfers between devices: 54 us -> 42.6 us  [butterfly(): values = values + lax.ppermute(values, axis, pairs)]
    another operation x0 -> x19, local copies, waits for them, and re-layouts: none -> 11.4 us  [the longest x6 4.7 us: apply_operator(): jnp.stack([outgoing_sides[None]] * lax.axis_size('brick'))]
    concatenate x14 -> x24, local copies, waits for them, and re-layouts: 20.6 us -> 25.5 us  [apply_operator(): jnp.concatenate([field[:, 1:, :], beyond_xplus[:, None, :]], axis=1)]
    concatenate x11 -> x18, local copies, waits for them, and re-layouts: 18.3 us -> 21.5 us  [apply_operator(): jnp.concatenate([beyond_xminus[:, None, :], field[:, :-1, :]], axis=1)]
  transfers between devices with their start and end apart: 58 -> 64, of which waited for: 34 -> 34; matrix products, arithmetic and copies ran while one was open for 30% -> 37% of each run, Pallas kernels for 0% -> 0%
where the time goes in v1:
time: 758 us; the launch traced here: 743 us
  local copies, waits for them, and re-layouts  329 us (43%)
  starting transfers between devices  188 us (25%)
  other arithmetic  154 us (20%)
  waiting for transfers between devices  42.6 us (6%)
  between operations  26.1 us (3%)
    ppermute x46, starting transfers between devices, butterfly(): values = values + lax.ppermute(values, axis, pairs)  139 us
    ppermute x46, waiting for transfers between devices, butterfly(): values = values + lax.ppermute(values, axis, pairs)  42.6 us
    broadcast_in_dim x26, local copies, waits for them, and re-layouts, apply_operator(): jnp.where(cube_third == BS - 1, from_above, jnp.roll(cube, -1, axis=3))  41.1 us
    broadcast_in_dim x26, local copies, waits for them, and re-layouts, apply_operator(): jnp.where(cube_third == 0, from_below, jnp.roll(cube, 1, axis=3))  40.3 us
    all_to_all x6, starting transfers between devices, apply_operator(): lax.all_to_all(jnp.stack([outgoing_sides[None]] * lax.axis_size('brick'))...  28.6 us
    concatenate x24, local copies, waits for them, and re-layouts, apply_operator(): jnp.concatenate([field[:, 1:, :], beyond_xplus[:, None, :]], axis=1)  25.5 us
    concatenate x12, local copies, waits for them, and re-layouts, apply_operator(): jnp.roll(cube, -1, axis=3)  24.2 us
    concatenate x12, local copies, waits for them, and re-layouts, apply_operator(): jnp.roll(cube, 1, axis=3)  24.2 us
  transfers between devices with their start and end apart: 64, of which 34 were waited for; matrix products, arithmetic and copies ran while one was open for 37% of the time, Pallas kernels for 0%

profile of v1, /device:TPU:0, one launch (start us, length us, event | category | flops | bytes accessed | tf_op | source)
XLA Modules:
  0.0 743.1 jit_solution(3721875262939553294)
XLA Ops:
  10.9 4.6 all-to-all-start
  42.1 5.5 multiply_divide_fusion.2
  71.6 5.6 collective-permute-start.3
  119.4 8.4 %fusion.46 = (f32[2,32,32,32]{3,2,1,0:T(8,128)S(1)}, f32[2,32,32,32]{3,2,1,0:T(8,128)}, f32[2,32,32,32]{3,2,1,0:T(8,128)}) fusion(f32[2,32,32,32]{3,2,1,0:T(8,128)} %get-tuple-element.67, f32[2,32,32,32]{3,2,1,0:T(8,128)} %copy-done.17, f32[2,32,32,32]{3,2,1,0:T(8,128)} %copy-done.16, f32[2,32,32,32]{3,2,1,0:T(8,128)} %concatenate.668, ...), kind=kLoop, calls=%fused_computation.88 | loop fusion | flops 2293760 | bytes 4538480 | tf_op jit(solution)/shard_map/add | solution.py:236
  150.2 4.8 all-to-all-start.1
  191.2 3.8 multiply_reduce_fusion.4
  219.6 4.7 collective-permute-start.20
  244.7 4.9 collective-permute-start.8
  256.3 3.8 collective-permute-done.10
  279.0 6.6 multiply_divide_fusion.1
  300.3 4.8 all-to-all-start.2
  349.6 3.7 multiply_reduce_fusion.3
  363.8 4.7 collective-permute-start.26
  369.7 3.8 collective-permute-start.27
  380.3 5.2 collective-permute-start.29
  386.5 4.7 collective-permute-start.30
  396.1 6.4 multiply_add_fusion.1
  408.0 4.8 all-to-all-start.3
  454.5 3.9 collective-permute-start.37
  460.0 5.5 collective-permute-start.38
  486.7 6.2 multiply_divide_fusion
  504.2 4.8 all-to-all-start.4
  551.7 3.9 multiply_reduce_fusion.1
  565.9 4.7 collective-permute-start.44
  571.6 3.8 collective-permute-start.45
  581.9 5.9 collective-permute-start.47
  588.6 4.4 collective-permute-start.48
  598.3 9.3 %multiply_add_fusion = f32[2,32,32,32]{3,2,1,0:T(8,128)S(1)} fusion(f32[2,32,32,32]{3,2,1,0:T(8,128)} %copy-done.18, f32[2,32,32,32]{3,2,1,0:T(8,128)} %get-tuple-element.67, f32[2,32,32,32]{3,2,1,0:T(8,128)} %copy-done.17, f32[2,32,32,32]{3,2,1,0:T(8,128)} %copy-done.16, f32[2,32,32,32]{3,2,1,0:T(8,128)} %concatenate.784, ...), kind=kLoop, calls=%fused_computation.76 | loop fusion | flops 3735552 | bytes 5865592 | tf_op jit(solution)/shard_map/add | solution.py:268
  613.4 4.8 all-to-all-start.5
  677.2 4.2 collective-permute-start.55
  681.5 3.9 fusion.96
  736.2 5.8 fusion.148
  (974 shorter events, 555.2 us)
Async XLA Ops:
  10.9 99.4 %all-to-all-start = ((f32[8,1,4,2,1024]{4,3,2,1,0:T(2,128)}), f32[8,1,4,2,1024]{4,3,2,1,0:T(2,128)}, u32[]{:S(2)}, u32[]{:S(2)}) async-start(f32[8,1,4,2,1024]{4,3,2,1,0:T(2,128)} %stack.143), calls=%async_computation | async-start | bytes 524288 | tf_op jit(solution)/shard_map/all_to_all | solution.py:123
  51.3 19.4 %collective-permute-start.2 = (f32[16,5,2]{2,0,1:T(8,128)}, f32[16,5,2]{2,0,1:T(8,128)}, u32[]{:S(2)}, u32[]{:S(2)}) collective-permute-start(f32[16,5,2]{2,0,1:T(8,128)} %broadcast_multiply_fusion.3), channel_id=1, source_target_pairs={{0,1},{1,0},{2,3},{3,2},{4,5},{5,4},{6,7},{7,6},{8,9},{9,8},{10,11... | collective-permute-start | bytes 1928 | tf_op jit(solution)/shard_map/ppermute | solution.py:203
  57.0 47.3 %collective-permute-start.1 = (f32[1,2,1024]{2,1,0:T(2,128)}, f32[1,2,1024]{2,1,0:T(2,128)}, u32[]{:S(2)}, u32[]{:S(2)}) collective-permute-start(f32[1,2,1024]{2,1,0:T(2,128)} %stack_reshape_squeeze.37), channel_id=1, source_target_pairs={{0,1},{1,2},{2,3},{3,4},{4,5},{5,6},{6,7},{7,8},{8,9},{9,10},{10,1... | collective-permute-start | bytes 24584 | tf_op jit(solution)/shard_map/ppermute | solution.py:18
  61.0 40.7 %collective-permute-start = (f32[1,2,1024]{2,1,0:T(2,128)}, f32[1,2,1024]{2,1,0:T(2,128)}, u32[]{:S(2)}, u32[]{:S(2)}) collective-permute-start(f32[1,2,1024]{2,1,0:T(2,128)} %stack_reshape_squeeze.36), channel_id=1, source_target_pairs={{1,0},{2,1},{3,2},{4,3},{5,4},{6,5},{7,6},{8,7},{9,8},{10,9},{11,1... | collective-permute-start | bytes 24584 | tf_op jit(solution)/shard_map/ppermute | solution.py:21
  71.6 7.5 %collective-permute-start.3 = (f32[16,5,2]{2,0,1:T(8,128)S(1)}, f32[16,5,2]{2,0,1:T(8,128)S(1)}, u32[]{:S(2)}, u32[]{:S(2)}) collective-permute-start(f32[16,5,2]{2,0,1:T(8,128)S(1)} %fusion.177), channel_id=1, source_target_pairs={{0,2},{1,3},{2,0},{3,1},{4,6},{5,7},{6,4},{7,5},{8,10},{9,11},{10,... | collective-permute-start | bytes 1928 | tf_op jit(solution)/shard_map/ppermute | solution.py:203
  85.6 7.6 %collective-permute-start.5 = (f32[16,5,2]{2,0,1:T(8,128)S(1)}, f32[16,5,2]{2,0,1:T(8,128)S(1)}, u32[]{:S(2)}, u32[]{:S(2)}) collective-permute-start(f32[16,5,2]{2,0,1:T(8,128)S(1)} %add.671), channel_id=1, source_target_pairs={{0,8},{1,9},{2,10},{3,11},{4,12},{5,13},{6,14},{7,15},{8,0},{9,1},... | collective-permute-start | bytes 1928 | tf_op jit(solution)/shard_map/ppermute | solution.py:203
  150.2 32.0 %all-to-all-start.1 = ((f32[8,1,4,2,1024]{4,3,2,1,0:T(2,128)}), f32[8,1,4,2,1024]{4,3,2,1,0:T(2,128)}, u32[]{:S(2)}, u32[]{:S(2)}) async-start(f32[8,1,4,2,1024]{4,3,2,1,0:T(2,128)} %stack.151), calls=%async_computation.1 | async-start | bytes 524288 | tf_op jit(solution)/shard_map/all_to_all | solution.py:123
  157.9 12.6 %collective-permute-start.14 = (f32[1,2,1024]{2,1,0:T(2,128)}, f32[1,2,1024]{2,1,0:T(2,128)}, u32[]{:S(2)}, u32[]{:S(2)}) collective-permute-start(f32[1,2,1024]{2,1,0:T(2,128)} %stack_reshape_squeeze.39), channel_id=1, source_target_pairs={{0,1},{1,2},{2,3},{3,4},{4,5},{5,6},{6,7},{7,8},{8,9},{9,10},{10,1... | collective-permute-start | bytes 24584 | tf_op jit(solution)/shard_map/ppermute | solution.py:18
  159.8 16.6 %collective-permute-start.13 = (f32[1,2,1024]{2,1,0:T(2,128)}, f32[1,2,1024]{2,1,0:T(2,128)}, u32[]{:S(2)}, u32[]{:S(2)}) collective-permute-start(f32[1,2,1024]{2,1,0:T(2,128)} %stack_reshape_squeeze.38), channel_id=1, source_target_pairs={{1,0},{2,1},{3,2},{4,3},{5,4},{6,5},{7,6},{8,7},{9,8},{10,9},{11,1... | collective-permute-start | bytes 24584 | tf_op jit(solution)/shard_map/ppermute | solution.py:21
  219.6 16.6 %collective-permute-start.20 = (f32[257]{0:T(512)}, f32[257]{0:T(512)}, u32[]{:S(2)}, u32[]{:S(2)}) collective-permute-start(f32[257]{0:T(512)} %add.700), channel_id=1, source_target_pairs={{0,4},{1,5},{2,6},{3,7},{4,0},{5,1},{6,2},{7,3},{8,12},{9,13},{10,... | collective-permute-start | bytes 3092 | tf_op jit(solution)/shard_map/ppermute | solution.py:203
  231.6 7.5 %collective-permute-start.6 = (f32[1]{0:T(128)}, f32[1]{0:T(128)}, u32[]{:S(2)}, u32[]{:S(2)}) collective-permute-start(f32[1]{0:T(128)} %bitcast.40), channel_id=1, source_target_pairs={{0,16},{16,0},{32,48},{48,32},{64,80},{80,64},{96,112},{112,96},{1... | collective-permute-start | bytes 20 | tf_op jit(solution)/shard_map/ppermute | solution.py:203
  237.0 34.4 %collective-permute-start.21 = (f32[257]{0:T(512)S(1)}, f32[257]{0:T(512)S(1)}, u32[]{:S(2)}, u32[]{:S(2)}) collective-permute-start(f32[257]{0:T(512)S(1)} %add.701), channel_id=1, source_target_pairs={{0,8},{1,9},{2,10},{3,11},{4,12},{5,13},{6,14},{7,15},{8,0},{9,1},... | collective-permute-start | bytes 3092 | tf_op jit(solution)/shard_map/ppermute | solution.py:203
  265.1 5.6 collective-permute-start.12
  300.3 37.6 %all-to-all-start.2 = ((f32[8,1,4,2,1024]{4,3,2,1,0:T(2,128)}), f32[8,1,4,2,1024]{4,3,2,1,0:T(2,128)}, u32[]{:S(2)}, u32[]{:S(2)}) async-start(f32[8,1,4,2,1024]{4,3,2,1,0:T(2,128)} %stack.157), calls=%async_computation.2 | async-start | bytes 524288 | tf_op jit(solution)/shard_map/all_to_all | solution.py:123
  308.0 18.2 %collective-permute-start.23 = (f32[1,2,1024]{2,1,0:T(2,128)}, f32[1,2,1024]{2,1,0:T(2,128)}, u32[]{:S(2)}, u32[]{:S(2)}) collective-permute-start(f32[1,2,1024]{2,1,0:T(2,128)} %stack_reshape_squeeze.41), channel_id=1, source_target_pairs={{0,1},{1,2},{2,3},{3,4},{4,5},{5,6},{6,7},{7,8},{8,9},{9,10},{10,1... | collective-permute-start | bytes 24584 | tf_op jit(solution)/shard_map/ppermute | solution.py:18
  310.5 21.5 %collective-permute-start.22 = (f32[1,2,1024]{2,1,0:T(2,128)}, f32[1,2,1024]{2,1,0:T(2,128)}, u32[]{:S(2)}, u32[]{:S(2)}) collective-permute-start(f32[1,2,1024]{2,1,0:T(2,128)} %stack_reshape_squeeze.40), channel_id=1, source_target_pairs={{1,0},{2,1},{3,2},{4,3},{5,4},{6,5},{7,6},{8,7},{9,8},{10,9},{11,1... | collective-permute-start | bytes 24584 | tf_op jit(solution)/shard_map/ppermute | solution.py:21
  408.0 24.3 %all-to-all-start.3 = ((f32[8,1,4,2,1024]{4,3,2,1,0:T(2,128)}), f32[8,1,4,2,1024]{4,3,2,1,0:T(2,128)}, u32[]{:S(2)}, u32[]{:S(2)}) async-start(f32[8,1,4,2,1024]{4,3,2,1,0:T(2,128)} %stack.163), calls=%async_computation.3 | async-start | bytes 524288 | tf_op jit(solution)/shard_map/all_to_all | solution.py:123
  413.6 11.2 %collective-permute-start.32 = (f32[1,2,1024]{2,1,0:T(2,128)S(1)}, f32[1,2,1024]{2,1,0:T(2,128)S(1)}, u32[]{:S(2)}, u32[]{:S(2)}) collective-permute-start(f32[1,2,1024]{2,1,0:T(2,128)S(1)} %stack_reshape_squeeze.43), channel_id=1, source_target_pairs={{0,1},{1,2},{2,3},{3,4},{4,5},{5,6},{6,7},{7,8},{8,9},{9,10},{10,1... | collective-permute-start | bytes 24584 | tf_op jit(solution)/shard_map/ppermute | solution.py:18
  415.8 12.0 %collective-permute-start.31 = (f32[1,2,1024]{2,1,0:T(2,128)}, f32[1,2,1024]{2,1,0:T(2,128)}, u32[]{:S(2)}, u32[]{:S(2)}) collective-permute-start(f32[1,2,1024]{2,1,0:T(2,128)} %stack_reshape_squeeze.42), channel_id=1, source_target_pairs={{1,0},{2,1},{3,2},{4,3},{5,4},{6,5},{7,6},{8,7},{9,8},{10,9},{11,1... | collective-permute-start | bytes 24584 | tf_op jit(solution)/shard_map/ppermute | solution.py:21
  460.0 7.1 collective-permute-start.38
  467.7 12.5 %collective-permute-start.39 = (f32[257]{0:T(512)}, f32[257]{0:T(512)}, u32[]{:S(2)}, u32[]{:S(2)}) collective-permute-start(f32[257]{0:T(512)} %add.733), channel_id=1, source_target_pairs={{0,8},{1,9},{2,10},{3,11},{4,12},{5,13},{6,14},{7,15},{8,0},{9,1},... | collective-permute-start | bytes 3092 | tf_op jit(solution)/shard_map/ppermute | solution.py:203
  504.2 35.7 %all-to-all-start.4 = ((f32[8,1,4,2,1024]{4,3,2,1,0:T(2,128)}), f32[8,1,4,2,1024]{4,3,2,1,0:T(2,128)}, u32[]{:S(2)}, u32[]{:S(2)}) async-start(f32[8,1,4,2,1024]{4,3,2,1,0:T(2,128)} %stack.169), calls=%async_computation.4 | async-start | bytes 524288 | tf_op jit(solution)/shard_map/all_to_all | solution.py:123
  511.3 17.6 %collective-permute-start.41 = (f32[1,2,1024]{2,1,0:T(2,128)S(1)}, f32[1,2,1024]{2,1,0:T(2,128)S(1)}, u32[]{:S(2)}, u32[]{:S(2)}) collective-permute-start(f32[1,2,1024]{2,1,0:T(2,128)S(1)} %stack_reshape_squeeze.45), channel_id=1, source_target_pairs={{0,1},{1,2},{2,3},{3,4},{4,5},{5,6},{6,7},{7,8},{8,9},{9,10},{10,1... | collective-permute-start | bytes 24584 | tf_op jit(solution)/shard_map/ppermute | solution.py:18
  513.2 20.9 %collective-permute-start.40 = (f32[1,2,1024]{2,1,0:T(2,128)}, f32[1,2,1024]{2,1,0:T(2,128)}, u32[]{:S(2)}, u32[]{:S(2)}) collective-permute-start(f32[1,2,1024]{2,1,0:T(2,128)} %stack_reshape_squeeze.44), channel_id=1, source_target_pairs={{1,0},{2,1},{3,2},{4,3},{5,4},{6,5},{7,6},{8,7},{9,8},{10,9},{11,1... | collective-permute-start | bytes 24584 | tf_op jit(solution)/shard_map/ppermute | solution.py:21
  581.9 6.1 collective-permute-start.47
  613.4 21.8 %all-to-all-start.5 = ((f32[8,1,4,2,1024]{4,3,2,1,0:T(2,128)}), f32[8,1,4,2,1024]{4,3,2,1,0:T(2,128)}, u32[]{:S(2)}, u32[]{:S(2)}) async-start(f32[8,1,4,2,1024]{4,3,2,1,0:T(2,128)} %stack.175), calls=%async_computation.5 | async-start | bytes 524288 | tf_op jit(solution)/shard_map/all_to_all | solution.py:123
  618.4 10.3 %collective-permute-start.50 = (f32[1,2,1024]{2,1,0:T(2,128)S(1)}, f32[1,2,1024]{2,1,0:T(2,128)S(1)}, u32[]{:S(2)}, u32[]{:S(2)}) collective-permute-start(f32[1,2,1024]{2,1,0:T(2,128)S(1)} %stack_reshape_squeeze.47), channel_id=1, source_target_pairs={{0,1},{1,2},{2,3},{3,4},{4,5},{5,6},{6,7},{7,8},{8,9},{9,10},{10,1... | collective-permute-start | bytes 24584 | tf_op jit(solution)/shard_map/ppermute | solution.py:18
  620.3 11.1 %collective-permute-start.49 = (f32[1,2,1024]{2,1,0:T(2,128)S(1)}, f32[1,2,1024]{2,1,0:T(2,128)S(1)}, u32[]{:S(2)}, u32[]{:S(2)}) collective-permute-start(f32[1,2,1024]{2,1,0:T(2,128)S(1)} %stack_reshape_squeeze.46), channel_id=1, source_target_pairs={{1,0},{2,1},{3,2},{4,3},{5,4},{6,5},{7,6},{8,7},{9,8},{10,9},{11,1... | collective-permute-start | bytes 24584 | tf_op jit(solution)/shard_map/ppermute | solution.py:21
  654.5 22.7 %collective-permute-start.54 = (f32[257]{0:T(512)S(1)}, f32[257]{0:T(512)S(1)}, u32[]{:S(2)}, u32[]{:S(2)}) collective-permute-start(f32[257]{0:T(512)S(1)} %add.758), channel_id=1, source_target_pairs={{0,1},{1,0},{2,3},{3,2},{4,5},{5,4},{6,7},{7,6},{8,9},{9,8},{10,11... | collective-permute-start | bytes 3092 | tf_op jit(solution)/shard_map/ppermute | solution.py:203
  677.2 8.1 %collective-permute-start.55 = (f32[257]{0:T(512)S(1)}, f32[257]{0:T(512)S(1)}, u32[]{:S(2)}, u32[]{:S(2)}) collective-permute-start(f32[257]{0:T(512)S(1)} %add.759), channel_id=1, source_target_pairs={{0,2},{1,3},{2,0},{3,1},{4,6},{5,7},{6,4},{7,5},{8,10},{9,11},{10,... | collective-permute-start | bytes 3092 | tf_op jit(solution)/shard_map/ppermute | solution.py:203
  685.9 23.5 %collective-permute-start.56 = (f32[257]{0:T(512)}, f32[257]{0:T(512)}, u32[]{:S(2)}, u32[]{:S(2)}) collective-permute-start(f32[257]{0:T(512)} %add.760), channel_id=1, source_target_pairs={{0,4},{1,5},{2,6},{3,7},{4,0},{5,1},{6,2},{7,3},{8,12},{9,13},{10,... | collective-permute-start | bytes 3092 | tf_op jit(solution)/shard_map/ppermute | solution.py:203
  710.7 23.5 %collective-permute-start.57 = (f32[257]{0:T(512)}, f32[257]{0:T(512)}, u32[]{:S(2)}, u32[]{:S(2)}) collective-permute-start(f32[257]{0:T(512)} %add.761), channel_id=1, source_target_pairs={{0,8},{1,9},{2,10},{3,11},{4,12},{5,13},{6,14},{7,15},{8,0},{9,1},... | collective-permute-start | bytes 3092 | tf_op jit(solution)/shard_map/ppermute | solution.py:203
  (249 other events, 1859.6 us)
